TPU v7x, 256 devices: a whole 4x4x8 slice. The times are simulated.
256 devices in a mesh: docs: 8 (over x, core), seq: 32 (over z, y).
Axes of the slice: x: 4, y: 4, z: 8, core: 2. Of those that a mesh axis runs over, the one named last changes fastest.
Arguments:
- byte_input: bfloat16 [81920, 256], P(('docs', 'seq')), parts along dimension 0, may hold values from -6 to 6
- w_short: bfloat16 [1024, 1024], replicated, may hold values from -0.1875 to 0.1875
- w_attend: bfloat16 [1024, 3072], replicated, may hold values from -0.1875 to 0.1875
- w_expand: bfloat16 [1024, 1024], replicated, may hold values from -0.75 to 0.75
- out_grad: bfloat16 [81920, 256], P(('docs', 'seq')), parts along dimension 0, may hold values from -6 to 6
Outputs:
- byte_output: bfloat16 [81920, 256], P(('docs', 'seq')), parts along dimension 0
- input_grad: bfloat16 [81920, 256], P(('docs', 'seq')), parts along dimension 0
- grad_short: float32 [8192, 1024], P(('docs', 'seq')), parts along dimension 0
- grad_attend: float32 [8192, 3072], P(('docs', 'seq')), parts along dimension 0
- grad_expand: float32 [8192, 1024], P(('docs', 'seq')), parts along dimension 0
There are 8 independent parts, one for each index of `docs`. A program takes and returns all parts, laid end to end along the dimension named above; an argument that names none is the same for every part. Nothing has to cross between parts.
All inputs are finite; a program needn't handle non-finite values.
Results may differ from a plain program's by a relative error of at most 0.028.
Values may be sent and summed in bfloat16 or wider, within the bound.
No kernel may reach another device: no remote copies, remote signals or barrier semaphores. Data moves between devices by JAX's collectives and lax.ppermute only.
A program may use at most 128 MiB of HBM per device.

v0:
```python
import jax
import jax.numpy as jnp
from jax import lax
from jax.sharding import PartitionSpec as P

HEADS = 8
SCORE_BOUND = 16.0
EPSILON = 1e-06


def from_behind(value, axis, steps):
    count = lax.axis_size(axis)
    leading, last = (max(0, -steps), min(count, count - steps))
    return lax.ppermute(value, axis, [(source, source + steps) for source in range(leading, last)])


def rounded(value):
    return lax.optimization_barrier(value.astype(jnp.bfloat16))


def unit_heads(matrix):
    split = matrix.reshape(matrix.shape[0], HEADS, -1)
    scale = lax.rsqrt(jnp.mean(split * split, axis=2, keepdims=True) + EPSILON)
    return (split * scale, scale)


def norm_back(normed, scale, upstream):
    inner = jnp.mean(normed * upstream, axis=2, keepdims=True)
    return scale * (upstream - normed * inner)


def powers_of(query3, key3, query_pos, key_pos, factor):
    dots = jnp.einsum("thd,rhd->htr", query3, key3, preferred_element_type=jnp.float32)
    live = query_pos[:, None] >= key_pos[None, :]
    return jnp.where(live[None], jnp.exp(dots * factor), 0.0)


def local(byte_input, w_short, w_attend, w_expand, out_grad):
    shard_count = lax.axis_size("seq")
    own_index = lax.axis_index("seq")
    short_rows = byte_input.shape[0] // 4
    byte_width = byte_input.shape[1]
    attn_width = w_attend.shape[1] // 3
    head_size = attn_width // HEADS
    factor = SCORE_BOUND / head_size
    first_pos = own_index * short_rows
    query_pos = first_pos + jnp.arange(short_rows, dtype=jnp.int32)
    group_shards = min(8, shard_count)
    group_rows = group_shards * short_rows
    turns = own_index // group_shards + 1
    edge = from_behind(byte_input[-3:], "seq", 1)
    grouped = jnp.concatenate([edge, byte_input[:-3]], axis=0).reshape(short_rows, 4 * byte_width)
    hidden = jnp.dot(grouped, w_short, preferred_element_type=jnp.float32)
    hidden_scale = lax.rsqrt(jnp.mean(hidden * hidden, axis=1, keepdims=True) + EPSILON)
    normed = hidden * hidden_scale
    normed_b = normed.astype(jnp.bfloat16)
    projected = jnp.dot(normed_b, w_attend, preferred_element_type=jnp.float32)
    query_unit, query_scale = unit_heads(projected[:, :attn_width])
    key_unit, key_scale = unit_heads(projected[:, attn_width : 2 * attn_width])
    query3 = query_unit.astype(jnp.bfloat16)
    key_own = key_unit.astype(jnp.bfloat16).reshape(short_rows, attn_width)
    value_own = projected[:, 2 * attn_width :].astype(jnp.bfloat16)
    pair = jnp.concatenate([key_own, value_own], axis=1)

    def unpack(block):
        rows = block.shape[0]
        keys3 = block[:, :attn_width].reshape(rows, HEADS, head_size)
        values3 = block[:, attn_width:].reshape(rows, HEADS, head_size)
        return (keys3, values3)

    def absorb(totals, block, key_first):
        weighted, denom = totals
        keys3, values3 = unpack(block)
        key_pos = key_first + jnp.arange(block.shape[0], dtype=jnp.int32)
        powers = powers_of(query3, keys3, query_pos, key_pos, factor)
        weighted = weighted + jnp.einsum(
            "htr,rhd->thd", powers.astype(jnp.bfloat16), values3, preferred_element_type=jnp.float32
        )
        denom = denom + jnp.sum(powers, axis=2).T
        return (weighted, denom)

    zero_query = jnp.zeros((short_rows, HEADS, head_size), jnp.float32)
    zero_denom = jnp.zeros((short_rows, HEADS), jnp.float32)
    keep = lax.all_gather(pair, "seq", axis=0, tiled=True)

    def forward_step(block_no, totals):
        key_first = block_no * group_rows
        return absorb(totals, lax.dynamic_slice_in_dim(keep, key_first, group_rows, 0), key_first)

    weighted, denom = lax.fori_loop(0, turns, forward_step, (zero_query, zero_denom))
    attended = rounded((weighted / denom[:, :, None]).reshape(short_rows, attn_width))
    expanded = jnp.dot(attended, w_expand, preferred_element_type=jnp.float32)
    byte_output = (
        byte_input.astype(jnp.float32) + expanded.reshape(4 * short_rows, byte_width)
    ).astype(jnp.bfloat16)
    d_expand = out_grad.reshape(short_rows, 4 * byte_width)
    d_attended = rounded(jnp.dot(d_expand, w_expand.T, preferred_element_type=jnp.float32))
    d_attended = d_attended.astype(jnp.float32).reshape(short_rows, HEADS, head_size)
    inverse = 1.0 / denom
    grad3 = (d_attended * inverse[:, :, None]).astype(jnp.bfloat16)
    attended_f = attended.astype(jnp.float32).reshape(short_rows, HEADS, head_size)
    shifts = (jnp.sum(d_attended * attended_f, axis=2) * inverse).astype(jnp.bfloat16)
    shifts_cols = shifts.astype(jnp.float32).T[:, :, None]

    def score_grads(keys3, values3, key_first):
        key_pos = key_first + jnp.arange(keys3.shape[0], dtype=jnp.int32)
        powers = powers_of(query3, keys3, query_pos, key_pos, factor)
        grad_dot = jnp.einsum("thd,rhd->htr", grad3, values3, preferred_element_type=jnp.float32)
        d_score = (powers * (grad_dot - shifts_cols) * factor).astype(jnp.bfloat16)
        return (powers, d_score)

    def backward_step(block_no, totals):
        query_grad, term = totals
        key_first = block_no * group_rows
        keys3, values3 = unpack(lax.dynamic_slice_in_dim(keep, key_first, group_rows, 0))
        powers, d_score = score_grads(keys3, values3, key_first)
        query_grad = query_grad + jnp.einsum(
            "htr,rhd->thd", d_score, keys3, preferred_element_type=jnp.float32
        )
        key_part = jnp.einsum(
            "htr,thd->rhd", d_score, query3, preferred_element_type=jnp.float32
        ).reshape(group_rows, attn_width)
        value_part = jnp.einsum(
            "htr,thd->rhd", powers.astype(jnp.bfloat16), grad3, preferred_element_type=jnp.float32
        ).reshape(group_rows, attn_width)
        term = lax.dynamic_update_slice_in_dim(
            term, jnp.concatenate([key_part, value_part], axis=1), key_first, 0
        )
        return (query_grad, term)

    empty_term = jnp.zeros((shard_count * short_rows, 2 * attn_width), jnp.float32)
    query_grad, term = lax.fori_loop(0, turns, backward_step, (zero_query, empty_term))
    key_values = lax.psum_scatter(
        term.astype(jnp.bfloat16), "seq", scatter_dimension=0, tiled=True
    ).astype(jnp.float32)
    key_grad = key_values[:, :attn_width].reshape(short_rows, HEADS, head_size)
    value_grad = key_values[:, attn_width:].reshape(short_rows, HEADS, head_size)
    d_query = norm_back(query_unit, query_scale, query_grad).reshape(short_rows, attn_width)
    d_key = norm_back(key_unit, key_scale, key_grad).reshape(short_rows, attn_width)
    d_projected = jnp.concatenate(
        [d_query, d_key, value_grad.reshape(short_rows, attn_width)], axis=1
    ).astype(jnp.bfloat16)
    d_normed = jnp.dot(d_projected, w_attend.T, preferred_element_type=jnp.float32)
    d_hidden = (
        hidden_scale * (d_normed - normed * jnp.mean(normed * d_normed, axis=1, keepdims=True))
    ).astype(jnp.bfloat16)
    d_grouped = (
        jnp.dot(d_hidden, w_short.T, preferred_element_type=jnp.float32)
        .astype(jnp.bfloat16)
        .reshape(4 * short_rows, byte_width)
    )
    back_edge = from_behind(d_grouped[:3], "seq", -1)
    moved = jnp.concatenate([d_grouped[3:], back_edge], axis=0).astype(jnp.float32)
    input_grad = (out_grad.astype(jnp.float32) + moved).astype(jnp.bfloat16)

    def part(left, right):
        return jnp.dot(left.T, right, preferred_element_type=jnp.float32)

    grads = lax.psum_scatter(
        jnp.concatenate(
            [part(grouped, d_hidden), part(normed_b, d_projected), part(attended, d_expand)], axis=1
        ).astype(jnp.bfloat16),
        "seq",
        scatter_dimension=0,
        tiled=True,
    ).astype(jnp.float32)
    model_width = w_short.shape[1]
    grad_short = grads[:, :model_width]
    grad_attend = grads[:, model_width : model_width + 3 * attn_width]
    grad_expand = grads[:, model_width + 3 * attn_width :]
    return (byte_output, input_grad, grad_short, grad_attend, grad_expand)


def solution(mesh):
    in_specs = (P(("docs", "seq"), None), P(), P(), P(), P(("docs", "seq"), None))
    out_specs = (
        P(("docs", "seq"), None),
        P(("docs", "seq"), None),
        P(("docs", "seq"), None),
        P(("docs", "seq"), None),
        P(("docs", "seq"), None),
    )
    return jax.shard_map(local, mesh=mesh, in_specs=in_specs, out_specs=out_specs, check_vma=False)
```

profile of v0, /device:TPU:2, one launch (start us, length us, event | category | flops | bytes accessed | tf_op | source)
XLA Modules:
  0.0 731.4 jit_solution(5632253812423761780)
XLA Ops:
  7.2 0.8 slice.53
  8.1 3.5 collective-permute-start
  11.5 1.3 collective-permute-done
  12.8 1.0 pad_maximum_fusion.6
  14.5 4.1 fusion.21
  18.6 0.7 slice.94
  19.7 0.7 copy-done.4
  20.9 0.7 copy-done.2
  21.6 1.2 slice_bitcast_fusion.1
  22.8 0.7 pad_maximum_fusion.3
  23.7 1.0 reshape.175
  24.7 2.4 convolution_convert_fusion.4
  27.1 0.8 convert_bitcast_fusion.1
  27.9 0.8 copy.114
  29.1 108.1 %all-gather.2.cloned.1.call-done = bf16[2560,2048]{1,0:T(8,128)(2,1)} async-done(((bf16[80,2048]{1,0:T(8,128)(2,1)}), bf16[2560,2048]{1,0:T(8,128)(2,1)}) %all-gather.2.cloned.1.call-update) | async-done | bytes 10485776 | tf_op jit(solution)/shard_map/all_gather | solution.py:84
  137.2 13.8 %copy.81 = bf16[2560,2048]{0,1:T(8,128)(2,1)} copy(bf16[2560,2048]{1,0:T(8,128)(2,1)} %all-gather.2.cloned.1.call-done) | data formatting | bytes 20971520
  151.0 3.5 while.26
  151.0 2.0 constant_dynamic-slice_fusion.3
  153.1 0.6 fusion.81
  153.8 0.7 fusion.82
  154.8 1.2 multiply_reduce_fusion.3
  156.2 5.2 broadcast_in_dim.51.clone
  161.4 14.7 %while.27 = (s32[]{:T(128)}, f32[80,8,128]{2,0,1:T(8,128)S(1)}, bf16[2560,2048]{1,0:T(8,128)(2,1)}, s32[]{:T(128)}, bf16[2560,2048]{0,1:T(8,128)(2,1)}, /*index=...) while((s32[]{:T(128)}, f32[80,8,128]{2,0,1:T(8,128)S(1)}, ...), condition=%wide.region_8.9_spmd.clone, body=%wide.region_7.8_spmd.clone.sunk | while | flops 532531936 | bytes 36319576 | solution.py:132
  161.4 1.9 fusion.93
  164.4 0.7 fusion.95
  166.2 1.8 pad_maximum_fusion.8
  168.0 4.5 copy.135
  172.5 3.6 constant_dynamic-update-slice_fusion.2
  176.7 0.9 copy_bitcast_fusion
  177.6 3.1 convolution_convert_fusion.1
  180.7 280.0 %reduce-scatter.3.cloned.1.call-done = bf16[80,2048]{1,0:T(8,128)(2,1)} async-done(((bf16[2560,2048]{1,0:T(8,128)(2,1)}), bf16[80,2048]{1,0:T(8,128)(2,1)}) %reduce-scatter.3.cloned.1.call-update) | async-done | bytes 327696 | tf_op jit(solution)/shard_map/reduce_scatter | solution.py:133
  460.7 1.0 convert_bitcast_fusion.2
  462.4 1.2 fusion.12
  463.6 4.9 multiply_reduce_fusion
  468.5 4.5 convolution_convert_fusion
  473.2 2.1 convolution_convert_fusion.2
  475.3 3.9 copy.91
  479.2 9.7 %pad_maximum_fusion.1 = bf16[1024,5120]{1,0:T(8,128)(2,1)} fusion(bf16[1024,1024]{1,0:T(8,128)(2,1)} %convolution_convert_fusion.1, bf16[1024,3072]{1,0:T(8,128)(2,1)} %convolution_convert_fusion, bf16[1024,1024]{1,0:T(8,128)(2,1)} %copy.91), kind=kLoop, calls=%fused_computation.25 | loop fusion | flops 31457280 | bytes 20971520 | tf_op jit(solution)/shard_map/concatenate | solution.py:160
  489.0 0.9 copy-done.7
  489.8 2.1 fusion.26
  492.0 0.8 convolution_convert_fusion.3
  492.9 1.3 collective-permute-start.1
  494.2 0.7 add_convert_fusion.1
  495.0 3.4 collective-permute-done.1
  498.4 0.7 add_convert_fusion
  499.1 222.5 %reduce-scatter.5.cloned.1.call-done = bf16[32,5120]{1,0:T(8,128)(2,1)} async-done(((bf16[1024,5120]{1,0:T(8,128)(2,1)}), bf16[32,5120]{1,0:T(8,128)(2,1)}) %reduce-scatter.5.cloned.1.call-update) | async-done | bytes 327696 | tf_op jit(solution)/shard_map/reduce_scatter | solution.py:159
  721.6 1.6 fusion.24
  723.2 1.7 slice.78
  (84 shorter events, 6.5 us)
Async XLA Ops:
  7.2 6.7 copy-start
  7.2 130.0 %all-gather.2.cloned.1.call-start = ((), (), s32[]{:S(2)}) async-start(), calls=%async_computation.2 | async-start | bytes 10813440 | tf_op jit(solution)/shard_map/all_gather | solution.py:84
  8.1 4.8 collective-permute-start
  13.9 4.7 copy-start.8
  18.6 1.0 copy-start.1
  19.6 3.2 copy-start.14
  19.7 0.7 copy-start.4
  20.9 0.7 copy-start.2
  23.6 437.1 %reduce-scatter.3.cloned.1.call-start = ((), (), s32[]{:S(2)}) async-start(), calls=%async_computation.3 | async-start | bytes 10813440 | tf_op jit(solution)/shard_map/reduce_scatter | solution.py:133
  24.7 4.0 copy-start.10
  154.6 1.4 copy-start.6
  154.6 1.4 copy-start.12
  176.1 545.5 %reduce-scatter.5.cloned.1.call-start = ((), (), s32[]{:S(2)}) async-start(), calls=%async_computation.4 | async-start | bytes 10813440 | tf_op jit(solution)/shard_map/reduce_scatter | solution.py:159
  177.6 284.2 %copy-start.5 = (f32[10,8,8,128]{3,2,1,0:T(8,128)S(1)}, f32[10,8,8,128]{3,2,1,0:T(8,128)}, u32[]{:S(2)}) copy-start(f32[10,8,8,128]{3,2,1,0:T(8,128)} %copy-done.4) | copy-start | bytes 983044
  177.6 284.8 %copy-start.3 = (f32[80,8,128]{2,1,0:T(8,128)S(1)}, f32[80,8,128]{2,1,0:T(8,128)}, u32[]{:S(2)}) copy-start(f32[80,8,128]{2,1,0:T(8,128)} %copy-done.2) | copy-start | bytes 983044
  180.7 282.9 %copy-start.11 = (bf16[80,1024]{1,0:T(8,128)(2,1)S(1)}, bf16[80,1024]{1,0:T(8,128)(2,1)}, u32[]{:S(2)}) copy-start(bf16[80,1024]{1,0:T(8,128)(2,1)} %copy_bitcast_fusion) | copy-start | bytes 491524
  468.5 4.6 copy-start.9
  488.9 0.9 copy-start.7
  491.9 2.3 copy-start.13
  491.9 6.5 copy-start.15
  492.9 5.5 collective-permute-start.1
Sparse Core Ops, SparseCore 0:
  23.7 113.4 all-gather.1
  176.2 284.4 reduce-scatter.2
  489.1 232.4 reduce-scatter.4
where the time goes:
time: 733 us; the launch traced here: 731 us
  waiting for transfers between devices  615 us (84%)
  local copies, waits for them, and re-layouts  45.6 us (6%)
  matrix products  28.5 us (4%)
  other arithmetic  22.7 us (3%)
  between operations  14.2 us (2%)
    reduce_scatter x1, waiting for transfers between devices, local(): lax.psum_scatter(term.astype(jnp.bfloat16), 'seq', scatter_dimension=0, t...  280 us
    reduce_scatter x1, waiting for transfers between devices, local(): lax.psum_scatter(jnp.concatenate([part(grouped, d_hidden), part(normed_b,...  222 us
    all_gather x1, waiting for transfers between devices, local(): keep = lax.all_gather(pair, 'seq', axis=0, tiled=True)  108 us
    unnamed x39, local copies, waits for them, and re-layouts  17.5 us
  transfers between devices with their start and end apart: 5, of which 5 were waited for; matrix products, arithmetic and copies ran while one was open for 2% of the time, Pallas kernels for 0%

commit v1 on v0

--- a/solution.py
+++ b/solution.py
@@ -81,7 +81,9 @@
 
     zero_query = jnp.zeros((short_rows, HEADS, head_size), jnp.float32)
     zero_denom = jnp.zeros((short_rows, HEADS), jnp.float32)
-    keep = lax.all_gather(pair, "seq", axis=0, tiled=True)
+    keep = jnp.concatenate(
+        lax.all_to_all(jnp.stack([pair] * lax.axis_size("seq")), "seq", 0, 0), axis=0
+    )
 
     def forward_step(block_no, totals):
         key_first = block_no * group_rows

time: 733 us -> 879 us (1.20)
  waiting for transfers between devices: 615 us -> 744 us
  starting transfers between devices: 5.06 us -> 18.1 us
    all_to_all x0 -> x1, waiting for transfers between devices: none -> 226 us  [local(): lax.all_to_all(jnp.stack([pair] * lax.axis_size('seq')), 'seq', 0, 0)]
    all_gather x1 -> x0, waiting for transfers between devices: 108 us -> none  [local(): keep = lax.all_gather(pair, 'seq', axis=0, tiled=True)]
    all_to_all x0 -> x1, starting transfers between devices: none -> 13.1 us  [local(): lax.all_to_all(jnp.stack([pair] * lax.axis_size('seq')), 'seq', 0, 0)]
    reduce_scatter x1, waiting for transfers between devices: 280 us -> 291 us  [local(): lax.psum_scatter(term.astype(jnp.bfloat16), 'seq', scatter_dimension=0, t...]
where the time goes in v1:
time: 879 us; the launch traced here: 878 us
  waiting for transfers between devices  744 us (85%)
  local copies, waits for them, and re-layouts  50 us (6%)
  matrix products  28.5 us (3%)
  other arithmetic  21.9 us (2%)
  starting transfers between devices  18.1 us (2%)
  between operations  14.5 us (2%)
    reduce_scatter x1, waiting for transfers between devices, local(): lax.psum_scatter(term.astype(jnp.bfloat16), 'seq', scatter_dimension=0, t...  291 us
    all_to_all x1, waiting for transfers between devices, local(): lax.all_to_all(jnp.stack([pair] * lax.axis_size('seq')), 'seq', 0, 0)  226 us
    reduce_scatter x1, waiting for transfers between devices, local(): lax.psum_scatter(jnp.concatenate([part(grouped, d_hidden), part(normed_b,...  223 us
  transfers between devices with their start and end apart: 5, of which 5 were waited for; matrix products, arithmetic and copies ran while one was open for 2% of the time, Pallas kernels for 0%

profile of v1, /device:TPU:2, one launch (start us, length us, event | category | flops | bytes accessed | tf_op | source)
XLA Modules:
  0.0 877.6 jit_solution(17153321744082066325)
XLA Ops:
  7.2 0.8 slice.53
  8.0 3.5 collective-permute-start
  11.5 1.3 collective-permute-done
  12.8 1.0 pad_maximum_fusion.6
  14.5 4.1 fusion.21
  18.6 0.7 slice.94
  19.7 0.7 copy-done.4
  20.9 0.7 copy-done.2
  21.6 1.2 slice_bitcast_fusion.1
  22.8 5.3 stack.2
  28.1 13.1 %all-to-all-start = ((bf16[32,80,2048]{2,1,0:T(8,128)(2,1)}), bf16[32,80,2048]{2,1,0:T(8,128)(2,1)}, u32[]{:S(2)}, u32[]{:S(2)}) async-start(bf16[32,80,2048]{2,1,0:T(8,128)(2,1)} %stack.2), calls=%async_computation | async-start | bytes 20971520 | tf_op jit(solution)/shard_map/all_to_all | solution.py:85
  41.4 2.4 convolution_convert_fusion.4
  43.9 0.8 convert_bitcast_fusion.1
  44.6 0.8 copy.129
  45.9 226.2 %all-to-all-done = bf16[32,80,2048]{2,1,0:T(8,128)(2,1)} async-done(((bf16[32,80,2048]{2,1,0:T(8,128)(2,1)}), bf16[32,80,2048]{2,1,0:T(8,128)(2,1)}, u32[]{:S(2)}, u32[]{:S(2)}) %all-to-all-start) | async-done | bytes 10485792 | tf_op jit(solution)/shard_map/all_to_all | solution.py:85
  272.1 13.8 %copy.96 = bf16[2560,2048]{0,1:T(8,128)(2,1)} copy(bf16[2560,2048]{1,0:T(8,128)(2,1)} %bitcast) | data formatting | bytes 20971520
  285.9 3.5 while.26
  286.0 2.0 constant_dynamic-slice_fusion.3
  288.0 0.6 fusion.81
  288.7 0.7 fusion.82
  289.7 1.2 multiply_reduce_fusion.3
  291.1 5.2 broadcast_in_dim.51.clone
  296.3 14.7 %while.27 = (s32[]{:T(128)}, f32[80,8,128]{2,0,1:T(8,128)S(1)}, bf16[2560,2048]{1,0:T(8,128)(2,1)}, s32[]{:T(128)}, bf16[2560,2048]{0,1:T(8,128)(2,1)}, /*index=...) while((s32[]{:T(128)}, f32[80,8,128]{2,0,1:T(8,128)S(1)}, ...), condition=%wide.region_8.9_spmd.clone, body=%wide.region_7.8_spmd.clone.sunk | while | flops 532531936 | bytes 36319576 | solution.py:134
  296.3 1.9 fusion.93
  299.3 0.7 fusion.95
  301.1 1.8 pad_maximum_fusion.8
  302.9 4.5 copy.150
  307.4 3.6 constant_dynamic-update-slice_fusion.2
  311.6 0.9 copy_bitcast_fusion
  312.6 3.1 convolution_convert_fusion.1
  315.7 290.6 %reduce-scatter.3.cloned.1.call-done = bf16[80,2048]{1,0:T(8,128)(2,1)} async-done(((bf16[2560,2048]{1,0:T(8,128)(2,1)}), bf16[80,2048]{1,0:T(8,128)(2,1)}) %reduce-scatter.3.cloned.1.call-update) | async-done | bytes 327696 | tf_op jit(solution)/shard_map/reduce_scatter | solution.py:135
  606.3 1.0 convert_bitcast_fusion.2
  608.0 1.2 fusion.12
  609.1 4.9 multiply_reduce_fusion
  614.1 4.5 convolution_convert_fusion
  618.7 2.1 convolution_convert_fusion.2
  620.8 3.9 copy.106
  624.7 9.7 %pad_maximum_fusion.1 = bf16[1024,5120]{1,0:T(8,128)(2,1)} fusion(bf16[1024,1024]{1,0:T(8,128)(2,1)} %convolution_convert_fusion.1, bf16[1024,3072]{1,0:T(8,128)(2,1)} %convolution_convert_fusion, bf16[1024,1024]{1,0:T(8,128)(2,1)} %copy.106), kind=kLoop, calls=%fused_computation.25 | loop fusion | flops 31457280 | bytes 20971520 | tf_op jit(solution)/shard_map/concatenate | solution.py:162
  634.5 0.9 copy-done.7
  635.4 2.1 fusion.26
  637.6 0.8 convolution_convert_fusion.3
  638.5 1.3 collective-permute-start.1
  639.8 0.7 add_convert_fusion.1
  640.5 3.4 collective-permute-done.1
  643.9 0.7 add_convert_fusion
  644.7 222.8 %reduce-scatter.5.cloned.1.call-done = bf16[32,5120]{1,0:T(8,128)(2,1)} async-done(((bf16[1024,5120]{1,0:T(8,128)(2,1)}), bf16[32,5120]{1,0:T(8,128)(2,1)}) %reduce-scatter.5.cloned.1.call-update) | async-done | bytes 327696 | tf_op jit(solution)/shard_map/reduce_scatter | solution.py:161
  867.4 1.6 fusion.24
  869.0 1.7 slice.78
  (86 shorter events, 6.6 us)
Async XLA Ops:
  7.2 6.7 copy-start
  8.0 4.8 collective-permute-start
  13.9 4.7 copy-start.8
  18.5 1.0 copy-start.1
  19.6 3.2 copy-start.14
  19.6 0.7 copy-start.4
  20.9 0.7 copy-start.2
  28.1 13.2 %copy-start.15 = (bf16[320,256]{1,0:T(8,128)(2,1)S(1)}, bf16[320,256]{1,0:T(8,128)(2,1)}, u32[]{:S(2)}) copy-start(bf16[320,256]{1,0:T(8,128)(2,1)} %param.13) | copy-start | bytes 491524
  28.1 244.0 %all-to-all-start = ((bf16[32,80,2048]{2,1,0:T(8,128)(2,1)}), bf16[32,80,2048]{2,1,0:T(8,128)(2,1)}, u32[]{:S(2)}, u32[]{:S(2)}) async-start(bf16[32,80,2048]{2,1,0:T(8,128)(2,1)} %stack.2), calls=%async_computation | async-start | bytes 20971520 | tf_op jit(solution)/shard_map/all_to_all | solution.py:85
  41.2 565.0 %reduce-scatter.3.cloned.1.call-start = ((), (), s32[]{:S(2)}) async-start(), calls=%async_computation.3 | async-start | bytes 10813440 | tf_op jit(solution)/shard_map/reduce_scatter | solution.py:135
  41.4 4.0 copy-start.10
  289.6 1.4 copy-start.6
  289.6 1.4 copy-start.12
  311.1 556.4 %reduce-scatter.5.cloned.1.call-start = ((), (), s32[]{:S(2)}) async-start(), calls=%async_computation.4 | async-start | bytes 10813440 | tf_op jit(solution)/shard_map/reduce_scatter | solution.py:161
  312.6 294.8 %copy-start.5 = (f32[10,8,8,128]{3,2,1,0:T(8,128)S(1)}, f32[10,8,8,128]{3,2,1,0:T(8,128)}, u32[]{:S(2)}) copy-start(f32[10,8,8,128]{3,2,1,0:T(8,128)} %copy-done.4) | copy-start | bytes 983044
  312.6 295.4 %copy-start.3 = (f32[80,8,128]{2,1,0:T(8,128)S(1)}, f32[80,8,128]{2,1,0:T(8,128)}, u32[]{:S(2)}) copy-start(f32[80,8,128]{2,1,0:T(8,128)} %copy-done.2) | copy-start | bytes 983044
  315.7 293.5 %copy-start.11 = (bf16[80,1024]{1,0:T(8,128)(2,1)S(1)}, bf16[80,1024]{1,0:T(8,128)(2,1)}, u32[]{:S(2)}) copy-start(bf16[80,1024]{1,0:T(8,128)(2,1)} %copy_bitcast_fusion) | copy-start | bytes 491524
  614.1 4.6 copy-start.9
  634.5 0.9 copy-start.7
  637.5 2.3 copy-start.13
  637.5 6.5 copy-start.16
  638.5 5.5 collective-permute-start.1
Sparse Core Ops, SparseCore 0:
  311.2 295.0 reduce-scatter.2
  634.6 232.7 reduce-scatter.4
